TPU v7x, 256 devices: a whole 4x4x8 slice. The times are simulated.
256 devices in a mesh: dom: 64 (over z, y, core), grp: 4 (over x).
Axes of the slice: x: 4, y: 4, z: 8, core: 2. Of those that a mesh axis runs over, the one named last changes fastest.
Arguments:
- element_faces: int32 [4, 8192], P(None, 'dom'), may hold values from 0 to 8191, as said below
- interior_load: bfloat16 [80, 8192], P(None, 'dom'), may hold values from -6 to 6
- inverses: bfloat16 [80, 80, 8192], P('grp', None, 'dom'), may hold values from -0.625 to 0.625
- lift_operator: float32 [80, 240], P('grp'), may hold values from -0.625 to 0.625
- face_area: float32 [4, 8192], P(None, 'dom'), may hold values from 0.3 to 27
- columns: int32 [7, 8192], P(None, 'dom'), may hold values from -1 to 8191, as said below
- blocks: float32 [7, 60, 60, 8192], P(None, 'grp', None, 'dom'), may hold values from -0.00119 to 0.00119
- diagonal: float32 [60, 8192], P('grp', 'dom'), may hold values from 1.02 to 1.3
Outputs:
- solution: float32 [60, 8192], P('grp', 'dom')
- residual: float32 [60, 8192], P('grp', 'dom')
Inputs may be any that keep to these rules, and one draw needn't show every extreme that they name: `element_faces`: every face block of an element is owned by the element's own index of dom or the one before or after it; an index owns the face blocks i * 128 to (i + 1) * 128 - 1. `columns`: slot 0 of a face block row holds the block itself. Every other nonnegative entry is a face block owned by the row's own index of dom or the one before or after it, and within one slot no number appears twice.
All inputs are finite; a program needn't handle non-finite values.
Results may differ from a plain program's by a relative error of at most 0.0003.
Values sent between devices are 32-bit elements; how exact they have to be, the bound alone decides.
A program may use at most 64 MiB of HBM per device.

v0:
```python
import jax
import jax.numpy as jnp
from jax import lax
from jax.sharding import Mesh
from jax.sharding import PartitionSpec as P

ITERS = 8
DOM = ("dom_0", "dom_1", "dom_2")
DOM_GRP = ("dom_0", "dom_1", "dom_2", "grp")


def in_order(blocks, dim):
    blocks = jnp.moveaxis(blocks, 0, dim)
    dims = blocks.shape
    return blocks.reshape(*dims[:dim], dims[dim] * dims[dim + 1], *dims[dim + 2 :])


def copy_for_each(value, axis):
    copies = jnp.broadcast_to(value, (lax.axis_size(axis), *value.shape))
    return lax.all_to_all(copies, axis, split_axis=0, concat_axis=0, tiled=True)


def gather_directly(value, axis, dim):
    return in_order(copy_for_each(value, axis), dim)


def padded(cells, sides, width):
    for axis, dim in sides:
        count = lax.axis_size(axis)
        ends = count - 1
        head = lax.slice_in_dim(cells, 0, width, axis=dim)
        tail = lax.slice_in_dim(cells, cells.shape[dim] - width, cells.shape[dim], axis=dim)
        cells = jnp.concatenate(
            [
                lax.ppermute(tail, axis, [(i, (i + 1) % count) for i in range(ends)]),
                cells,
                lax.ppermute(head, axis, [((i + 1) % count, i) for i in range(ends)]),
            ],
            axis=dim,
        )
    return cells


def shifted(block, axis, distance):
    devices = range(lax.axis_size(axis))
    route = [(i - distance, i) for i in devices if i - distance in devices]
    return lax.ppermute(block, axis, route)


def cut_along(value, dim, count):
    before, after = (value.shape[:dim], value.shape[dim + 1 :])
    return jnp.moveaxis(value.reshape(*before, count, -1, *after), dim, 0)


def summed_on_arrival(value, axis, dim):
    count = lax.axis_size(axis)
    blocks = lax.all_to_all(cut_along(value, dim, count), axis, 0, 0, tiled=True)
    return jnp.sum(blocks, axis=0)


def by_axis(value, axes):
    for axis in axes:
        value = lax.psum(value, axis)
    return value


def spread(field_rows):
    faces_here = field_rows.shape[1]
    whole = gather_directly(field_rows, "grp", 0)
    return padded(whole, ((DOM, 1),), faces_here)


def deliver(slab):
    faces_here = slab.shape[1] // 3
    from_upper = shifted(slab[:, :faces_here], DOM, -1)
    from_lower = shifted(slab[:, 2 * faces_here :], DOM, 1)
    summed = slab[:, faces_here : 2 * faces_here] + from_upper + from_lower
    return summed_on_arrival(summed, "grp", 0)


def to_slab(entries, targets, faces_here):
    return jax.ops.segment_sum(entries, targets.reshape(-1), num_segments=3 * faces_here).T


def operate(field_rows, blocks, local_index, usable, diagonal):
    slab = spread(field_rows)
    picked = jnp.where(usable[None, :, :], slab[:, local_index], jnp.zeros((), jnp.float32))
    forward = jnp.einsum("sijf,jsf->if", blocks, picked, precision=lax.Precision.HIGHEST)
    transposed = jnp.einsum("sijf,if->sjf", blocks, field_rows, precision=lax.Precision.HIGHEST)
    transposed = jnp.where(usable[:, None, :], transposed, jnp.zeros((), jnp.float32))
    slot_count, height, faces_here = transposed.shape
    entries = jnp.transpose(transposed, (0, 2, 1)).reshape(slot_count * faces_here, height)
    return diagonal * field_rows + forward + deliver(to_slab(entries, local_index, faces_here))


def two_products(residual, image):
    return (
        by_axis(jnp.sum(residual * residual), DOM_GRP),
        by_axis(jnp.sum(residual * image), DOM_GRP),
    )


def on_device(
    element_faces, interior_load, inverses, lift_operator, face_area, columns, blocks, diagonal
):
    domain = lax.axis_index(DOM)
    faces_here = diagonal.shape[1]
    full_width = lift_operator.shape[1] // 4
    elements_here = interior_load.shape[1]
    u_rows = jnp.einsum("ije,je->ie", inverses, interior_load, preferred_element_type=jnp.float32)
    lifted = lax.dot_general(
        lift_operator, u_rows, (((0,), (0,)), ((), ())), precision=lax.Precision.HIGHEST
    )
    contrib = -(lifted.reshape(4, full_width, elements_here) * face_area[:, None, :])
    entries = jnp.transpose(contrib, (0, 2, 1)).reshape(4 * elements_here, full_width)
    slot_faces = element_faces - (domain - 1) * faces_here
    right_side = deliver(to_slab(entries, slot_faces, faces_here))
    usable = columns >= 0
    local_index = jnp.where(usable, columns - (domain - 1) * faces_here, faces_here)
    solution = jnp.zeros_like(right_side)
    residual = right_side
    image = operate(residual, blocks, local_index, usable, diagonal)
    norm_now, product_sum = two_products(residual, image)
    alpha = norm_now / product_sum
    direction, along = (residual, image)
    for iteration in range(ITERS):
        solution = solution + alpha * direction
        residual = residual - alpha * along
        if iteration + 1 < ITERS:
            image = operate(residual, blocks, local_index, usable, diagonal)
            norm_next, product_sum = two_products(residual, image)
            ratio = norm_next / norm_now
            alpha = norm_next / (product_sum - ratio * norm_next / alpha)
            direction = residual + ratio * direction
            along = image + ratio * along
            norm_now = norm_next
    return (solution, residual)


def solution(mesh):
    torus = Mesh(
        mesh.devices.reshape(8, 4, 2, mesh.shape["grp"]), ("dom_0", "dom_1", "dom_2", "grp")
    )
    placed = (
        P(None, DOM),
        P(None, DOM),
        P("grp", None, DOM),
        P("grp", None),
        P(None, DOM),
        P(None, DOM),
        P(None, "grp", None, DOM),
        P("grp", DOM),
    )
    return jax.shard_map(
        on_device,
        mesh=torus,
        in_specs=placed,
        out_specs=(P("grp", DOM), P("grp", DOM)),
        check_vma=False,
    )
```

profile of v0, /device:TPU:8, one launch (start us, length us, event | category | flops | bytes accessed | tf_op | source)
XLA Modules:
  0.0 880.3 jit_solution(18303853080815893465)
XLA Ops:
  15.6 3.7 all-to-all-start
  20.0 4.8 all-to-all-done
  25.4 3.3 all-to-all-start.1
  28.6 5.4 all-to-all-done.1
  44.2 3.7 gather_fusion
  53.7 7.1 scatter_custom_fusion.1
  77.8 4.0 all-to-all-done.2
  82.5 25.4 %all-reduce.7 = (f32[]{:T(128)}, f32[]{:T(128)}) all-reduce(f32[]{:T(128)} %get-tuple-element.17, f32[]{:T(128)} %get-tuple-element.16), channel_id=1, replica_groups=mesh['dom_0'=8,'dom_1'=4,'dom_2'=2,'grp'=4] {'dom_0'}, use_global_device_ids=true, to_apply=%region_3.4 | all-reduce | flops 2 | bytes 16 | tf_op jit(solution)/shard_map/psum | solution.py:63
  107.9 13.2 %all-reduce.23 = (f32[]{:T(128)}, f32[]{:T(128)}) all-reduce(f32[]{:T(128)} %get-tuple-element.32, f32[]{:T(128)} %get-tuple-element.33), channel_id=1, replica_groups=mesh['dom_0'=8,'dom_1'=4,'dom_2'=2,'grp'=4] {'dom_1'}, use_global_device_ids=true, to_apply=%region_4.5 | all-reduce | flops 2 | bytes 16 | tf_op jit(solution)/shard_map/psum | solution.py:63
  124.2 9.5 %all-reduce.15 = (f32[]{:T(128)}, f32[]{:T(128)}) all-reduce(f32[]{:T(128)} %get-tuple-element.80, f32[]{:T(128)} %get-tuple-element.81), channel_id=1, replica_groups=mesh['dom_0'=8,'dom_1'=4,'dom_2'=2,'grp'=4] {'grp'}, use_global_device_ids=true, to_apply=%region_6.7 | all-reduce | flops 2 | bytes 16 | tf_op jit(solution)/shard_map/psum | solution.py:63
  135.0 8.5 all_to_all.85
  153.5 3.7 gather_fusion.1
  163.1 7.1 scatter_custom_fusion.2
  186.2 4.1 all-to-all-done.4
  190.9 17.9 %all-reduce.6 = (f32[]{:T(128)}, f32[]{:T(128)}) all-reduce(f32[]{:T(128)} %get-tuple-element.15, f32[]{:T(128)} %get-tuple-element.14), channel_id=1, replica_groups=mesh['dom_0'=8,'dom_1'=4,'dom_2'=2,'grp'=4] {'dom_0'}, use_global_device_ids=true, to_apply=%region_15.16 | all-reduce | flops 2 | bytes 16 | tf_op jit(solution)/shard_map/psum | solution.py:63
  208.8 12.1 %all-reduce.22 = (f32[]{:T(128)}, f32[]{:T(128)}) all-reduce(f32[]{:T(128)} %get-tuple-element.30, f32[]{:T(128)} %get-tuple-element.31), channel_id=1, replica_groups=mesh['dom_0'=8,'dom_1'=4,'dom_2'=2,'grp'=4] {'dom_1'}, use_global_device_ids=true, to_apply=%region_16.17 | all-reduce | flops 2 | bytes 16 | tf_op jit(solution)/shard_map/psum | solution.py:63
  224.1 9.6 %all-reduce.14 = (f32[]{:T(128)}, f32[]{:T(128)}) all-reduce(f32[]{:T(128)} %get-tuple-element.78, f32[]{:T(128)} %get-tuple-element.79), channel_id=1, replica_groups=mesh['dom_0'=8,'dom_1'=4,'dom_2'=2,'grp'=4] {'grp'}, use_global_device_ids=true, to_apply=%region_18.19 | all-reduce | flops 2 | bytes 16 | tf_op jit(solution)/shard_map/psum | solution.py:63
  238.1 8.5 all_to_all.86
  256.6 3.7 gather_fusion.2
  266.2 7.1 scatter_custom_fusion.3
  289.3 4.1 all-to-all-done.6
  295.3 17.8 %all-reduce.5 = (f32[]{:T(128)}, f32[]{:T(128)}) all-reduce(f32[]{:T(128)} %get-tuple-element.13, f32[]{:T(128)} %get-tuple-element.12), channel_id=1, replica_groups=mesh['dom_0'=8,'dom_1'=4,'dom_2'=2,'grp'=4] {'dom_0'}, use_global_device_ids=true, to_apply=%region_27.28 | all-reduce | flops 2 | bytes 16 | tf_op jit(solution)/shard_map/psum | solution.py:63
  313.1 12.1 %all-reduce.21 = (f32[]{:T(128)}, f32[]{:T(128)}) all-reduce(f32[]{:T(128)} %get-tuple-element.28, f32[]{:T(128)} %get-tuple-element.29), channel_id=1, replica_groups=mesh['dom_0'=8,'dom_1'=4,'dom_2'=2,'grp'=4] {'dom_1'}, use_global_device_ids=true, to_apply=%region_28.29 | all-reduce | flops 2 | bytes 16 | tf_op jit(solution)/shard_map/psum | solution.py:63
  328.4 9.5 %all-reduce.13 = (f32[]{:T(128)}, f32[]{:T(128)}) all-reduce(f32[]{:T(128)} %get-tuple-element.76, f32[]{:T(128)} %get-tuple-element.77), channel_id=1, replica_groups=mesh['dom_0'=8,'dom_1'=4,'dom_2'=2,'grp'=4] {'grp'}, use_global_device_ids=true, to_apply=%region_30.31 | all-reduce | flops 2 | bytes 16 | tf_op jit(solution)/shard_map/psum | solution.py:63
  342.4 8.5 all_to_all.87
  362.2 3.7 gather_fusion.3
  371.8 7.1 scatter_custom_fusion.4
  391.6 3.9 all-to-all-start.8
  396.8 4.2 all-to-all-done.8
  402.4 17.8 %all-reduce.4 = (f32[]{:T(128)}, f32[]{:T(128)}) all-reduce(f32[]{:T(128)} %get-tuple-element.11, f32[]{:T(128)} %get-tuple-element.10), channel_id=1, replica_groups=mesh['dom_0'=8,'dom_1'=4,'dom_2'=2,'grp'=4] {'dom_0'}, use_global_device_ids=true, to_apply=%region_39.40 | all-reduce | flops 2 | bytes 16 | tf_op jit(solution)/shard_map/psum | solution.py:63
  420.2 12.1 %all-reduce.20 = (f32[]{:T(128)}, f32[]{:T(128)}) all-reduce(f32[]{:T(128)} %get-tuple-element.26, f32[]{:T(128)} %get-tuple-element.27), channel_id=1, replica_groups=mesh['dom_0'=8,'dom_1'=4,'dom_2'=2,'grp'=4] {'dom_1'}, use_global_device_ids=true, to_apply=%region_40.41 | all-reduce | flops 2 | bytes 16 | tf_op jit(solution)/shard_map/psum | solution.py:63
  435.4 9.6 %all-reduce.12 = (f32[]{:T(128)}, f32[]{:T(128)}) all-reduce(f32[]{:T(128)} %get-tuple-element.74, f32[]{:T(128)} %get-tuple-element.75), channel_id=1, replica_groups=mesh['dom_0'=8,'dom_1'=4,'dom_2'=2,'grp'=4] {'grp'}, use_global_device_ids=true, to_apply=%region_42.43 | all-reduce | flops 2 | bytes 16 | tf_op jit(solution)/shard_map/psum | solution.py:63
  448.9 8.5 all_to_all.88
  468.7 3.7 gather_fusion.4
  478.2 7.1 scatter_custom_fusion.5
  498.1 3.9 all-to-all-start.10
  503.3 4.2 all-to-all-done.10
  508.9 17.8 %all-reduce.3 = (f32[]{:T(128)}, f32[]{:T(128)}) all-reduce(f32[]{:T(128)} %get-tuple-element.9, f32[]{:T(128)} %get-tuple-element.8), channel_id=1, replica_groups=mesh['dom_0'=8,'dom_1'=4,'dom_2'=2,'grp'=4] {'dom_0'}, use_global_device_ids=true, to_apply=%region_51.52 | all-reduce | flops 2 | bytes 16 | tf_op jit(solution)/shard_map/psum | solution.py:63
  526.7 12.1 %all-reduce.19 = (f32[]{:T(128)}, f32[]{:T(128)}) all-reduce(f32[]{:T(128)} %get-tuple-element.24, f32[]{:T(128)} %get-tuple-element.25), channel_id=1, replica_groups=mesh['dom_0'=8,'dom_1'=4,'dom_2'=2,'grp'=4] {'dom_1'}, use_global_device_ids=true, to_apply=%region_52.53 | all-reduce | flops 2 | bytes 16 | tf_op jit(solution)/shard_map/psum | solution.py:63
  542.0 9.5 %all-reduce.11 = (f32[]{:T(128)}, f32[]{:T(128)}) all-reduce(f32[]{:T(128)} %get-tuple-element.72, f32[]{:T(128)} %get-tuple-element.73), channel_id=1, replica_groups=mesh['dom_0'=8,'dom_1'=4,'dom_2'=2,'grp'=4] {'grp'}, use_global_device_ids=true, to_apply=%region_54.55 | all-reduce | flops 2 | bytes 16 | tf_op jit(solution)/shard_map/psum | solution.py:63
  556.0 8.5 all_to_all.89
  575.8 3.7 gather_fusion.5
  585.4 7.1 scatter_custom_fusion.6
  605.2 3.9 all-to-all-start.12
  610.4 4.2 all-to-all-done.12
  617.3 17.8 %all-reduce.2 = (f32[]{:T(128)}, f32[]{:T(128)}) all-reduce(f32[]{:T(128)} %get-tuple-element.7, f32[]{:T(128)} %get-tuple-element.6), channel_id=1, replica_groups=mesh['dom_0'=8,'dom_1'=4,'dom_2'=2,'grp'=4] {'dom_0'}, use_global_device_ids=true, to_apply=%region_63.64 | all-reduce | flops 2 | bytes 16 | tf_op jit(solution)/shard_map/psum | solution.py:63
  635.1 12.1 %all-reduce.18 = (f32[]{:T(128)}, f32[]{:T(128)}) all-reduce(f32[]{:T(128)} %get-tuple-element.22, f32[]{:T(128)} %get-tuple-element.23), channel_id=1, replica_groups=mesh['dom_0'=8,'dom_1'=4,'dom_2'=2,'grp'=4] {'dom_1'}, use_global_device_ids=true, to_apply=%region_64.65 | all-reduce | flops 2 | bytes 16 | tf_op jit(solution)/shard_map/psum | solution.py:63
  650.3 9.5 %all-reduce.10 = (f32[]{:T(128)}, f32[]{:T(128)}) all-reduce(f32[]{:T(128)} %get-tuple-element.70, f32[]{:T(128)} %get-tuple-element.71), channel_id=1, replica_groups=mesh['dom_0'=8,'dom_1'=4,'dom_2'=2,'grp'=4] {'grp'}, use_global_device_ids=true, to_apply=%region_66.67 | all-reduce | flops 2 | bytes 16 | tf_op jit(solution)/shard_map/psum | solution.py:63
  663.5 8.5 all_to_all.90
  683.4 3.7 gather_fusion.6
  692.9 7.1 scatter_custom_fusion.7
  712.8 3.9 all-to-all-start.14
  718.0 4.2 all-to-all-done.14
  723.6 17.8 %all-reduce.1 = (f32[]{:T(128)}, f32[]{:T(128)}) all-reduce(f32[]{:T(128)} %get-tuple-element.5, f32[]{:T(128)} %get-tuple-element.4), channel_id=1, replica_groups=mesh['dom_0'=8,'dom_1'=4,'dom_2'=2,'grp'=4] {'dom_0'}, use_global_device_ids=true, to_apply=%region_75.76 | all-reduce | flops 2 | bytes 16 | tf_op jit(solution)/shard_map/psum | solution.py:63
  741.4 12.1 %all-reduce.17 = (f32[]{:T(128)}, f32[]{:T(128)}) all-reduce(f32[]{:T(128)} %get-tuple-element.20, f32[]{:T(128)} %get-tuple-element.21), channel_id=1, replica_groups=mesh['dom_0'=8,'dom_1'=4,'dom_2'=2,'grp'=4] {'dom_1'}, use_global_device_ids=true, to_apply=%region_76.77 | all-reduce | flops 2 | bytes 16 | tf_op jit(solution)/shard_map/psum | solution.py:63
  756.6 9.5 %all-reduce.9 = (f32[]{:T(128)}, f32[]{:T(128)}) all-reduce(f32[]{:T(128)} %get-tuple-element.68, f32[]{:T(128)} %get-tuple-element.69), channel_id=1, replica_groups=mesh['dom_0'=8,'dom_1'=4,'dom_2'=2,'grp'=4] {'grp'}, use_global_device_ids=true, to_apply=%region_78.79 | all-reduce | flops 2 | bytes 16 | tf_op jit(solution)/shard_map/psum | solution.py:63
  770.7 8.5 all_to_all.91
  790.5 3.7 gather_fusion.7
  800.1 7.1 scatter_custom_fusion.8
  819.9 3.9 all-to-all-start.16
  825.7 3.6 all-to-all-done.16
  831.4 17.8 %all-reduce = (f32[]{:T(128)}, f32[]{:T(128)}) all-reduce(f32[]{:T(128)} %get-tuple-element.3, f32[]{:T(128)} %get-tuple-element.2), channel_id=1, replica_groups=mesh['dom_0'=8,'dom_1'=4,'dom_2'=2,'grp'=4] {'dom_0'}, use_global_device_ids=true, to_apply=%region_87.88 | all-reduce | flops 2 | bytes 16 | tf_op jit(solution)/shard_map/psum | solution.py:63
  849.2 12.1 %all-reduce.16 = (f32[]{:T(128)}, f32[]{:T(128)}) all-reduce(f32[]{:T(128)} %get-tuple-element.18, f32[]{:T(128)} %get-tuple-element.19), channel_id=1, replica_groups=mesh['dom_0'=8,'dom_1'=4,'dom_2'=2,'grp'=4] {'dom_1'}, use_global_device_ids=true, to_apply=%region_88.89 | all-reduce | flops 2 | bytes 16 | tf_op jit(solution)/shard_map/psum | solution.py:63
  864.5 9.6 %all-reduce.8 = (f32[]{:T(128)}, f32[]{:T(128)}) all-reduce(f32[]{:T(128)} %get-tuple-element.66, f32[]{:T(128)} %get-tuple-element.67), channel_id=1, replica_groups=mesh['dom_0'=8,'dom_1'=4,'dom_2'=2,'grp'=4] {'grp'}, use_global_device_ids=true, to_apply=%region_90.91 | all-reduce | flops 2 | bytes 16 | tf_op jit(solution)/shard_map/psum | solution.py:63
  (266 shorter events, 311.4 us)
Async XLA Ops:
  0.6 1.9 copy-start
  6.8 5.0 collective-permute-start
  8.7 6.1 collective-permute-start.1
  11.8 151.2 %copy-start.16 = (s32[896]{0:T(1024)}, s32[896]{0:T(1024)S(1)}, u32[]{:S(2)}) copy-start(s32[896]{0:T(1024)S(1)} %get-tuple-element.109) | copy-start | bytes 10756
  15.6 9.2 %all-to-all-start = ((f32[4,15,128]{2,1,0:T(8,128)}), f32[4,15,128]{2,1,0:T(8,128)S(1)}, u32[]{:S(2)}, u32[]{:S(2)}) async-start(f32[4,15,128]{2,1,0:T(8,128)} %reshape.90), calls=%async_computation | async-start | bytes 65536 | tf_op jit(solution)/shard_map/all_to_all | solution.py:57
  25.4 8.7 all-to-all-start.1
  34.8 7.4 collective-permute-start.3
  36.7 5.8 collective-permute-start.2
  42.2 34.2 %copy-start.1 = (f32[7,15,60,128]{3,2,1,0:T(8,128)S(1)}, f32[7,15,60,128]{3,2,1,0:T(8,128)}, u32[]{:S(2)}) copy-start(f32[7,15,60,128]{3,2,1,0:T(8,128)} %param.14) | copy-start | bytes 9676804
  49.8 32.1 %copy-start.2 = (f32[15,128]{1,0:T(8,128)S(1)}, f32[15,128]{1,0:T(8,128)}, u32[]{:S(2)}) copy-start(f32[15,128]{1,0:T(8,128)} %param.15) | copy-start | bytes 23044
  61.7 6.5 collective-permute-start.4
  64.5 5.6 collective-permute-start.5
  73.2 8.7 all-to-all-start.2
  145.0 7.8 copy-start.3
  145.0 5.6 collective-permute-start.7
  147.0 5.8 collective-permute-start.6
  171.0 6.5 collective-permute-start.8
  172.9 5.6 collective-permute-start.9
  181.5 8.7 all-to-all-start.4
  190.9 71.3 %copy-start.13 = (f32[15,128]{1,0:T(8,128)}, f32[15,128]{1,0:T(8,128)S(1)}, u32[]{:S(2)}) copy-start(f32[15,128]{1,0:T(8,128)S(1)} %get-tuple-element.88) | copy-start | bytes 23044
  248.1 7.8 copy-start.4
  248.1 5.6 collective-permute-start.11
  250.1 5.8 collective-permute-start.10
  274.1 6.0 collective-permute-start.12
  276.0 5.6 collective-permute-start.13
  284.7 8.7 all-to-all-start.6
  342.4 106.5 %copy-start.15 = (f32[15,128]{1,0:T(8,128)}, f32[15,128]{1,0:T(8,128)S(1)}, u32[]{:S(2)}) copy-start(f32[15,128]{1,0:T(8,128)S(1)} %get-tuple-element.87) | copy-start | bytes 23044
  353.7 7.8 copy-start.5
  353.7 5.6 collective-permute-start.15
  355.7 5.8 collective-permute-start.14
  379.7 6.0 collective-permute-start.16
  381.6 5.6 collective-permute-start.17
  391.6 9.4 %all-to-all-start.8 = ((f32[4,15,128]{2,1,0:T(8,128)}), f32[4,15,128]{2,1,0:T(8,128)}, u32[]{:S(2)}, u32[]{:S(2)}) async-start(f32[4,15,128]{2,1,0:T(8,128)} %reshape.102), calls=%async_computation.8 | async-start | bytes 65536 | tf_op jit(solution)/shard_map/all_to_all | solution.py:57
  460.2 7.8 copy-start.6
  460.2 5.7 collective-permute-start.19
  462.2 5.8 collective-permute-start.18
  486.2 6.0 collective-permute-start.20
  488.1 5.6 collective-permute-start.21
  498.1 9.4 %all-to-all-start.10 = ((f32[4,15,128]{2,1,0:T(8,128)}), f32[4,15,128]{2,1,0:T(8,128)}, u32[]{:S(2)}, u32[]{:S(2)}) async-start(f32[4,15,128]{2,1,0:T(8,128)} %reshape.105), calls=%async_computation.10 | async-start | bytes 65536 | tf_op jit(solution)/shard_map/all_to_all | solution.py:57
  508.2 46.4 %copy-start.14 = (f32[15,128]{1,0:T(8,128)}, f32[15,128]{1,0:T(8,128)S(1)}, u32[]{:S(2)}) copy-start(f32[15,128]{1,0:T(8,128)S(1)} %reduce_sum.239) | copy-start | bytes 23044
  556.0 107.5 %copy-start.12 = (f32[15,128]{1,0:T(8,128)}, f32[15,128]{1,0:T(8,128)S(1)}, u32[]{:S(2)}) copy-start(f32[15,128]{1,0:T(8,128)S(1)} %get-tuple-element.84) | copy-start | bytes 23044
  567.3 7.8 copy-start.7
  567.3 5.6 collective-permute-start.23
  569.3 5.8 collective-permute-start.22
  593.3 6.0 collective-permute-start.24
  595.2 5.6 collective-permute-start.25
  605.2 9.4 %all-to-all-start.12 = ((f32[4,15,128]{2,1,0:T(8,128)}), f32[4,15,128]{2,1,0:T(8,128)}, u32[]{:S(2)}, u32[]{:S(2)}) async-start(f32[4,15,128]{2,1,0:T(8,128)} %reshape.108), calls=%async_computation.12 | async-start | bytes 65536 | tf_op jit(solution)/shard_map/all_to_all | solution.py:57
  617.3 71.7 %copy-start.10 = (f32[15,128]{1,0:T(8,128)}, f32[15,128]{1,0:T(8,128)S(1)}, u32[]{:S(2)}) copy-start(f32[15,128]{1,0:T(8,128)S(1)} %get-tuple-element.82) | copy-start | bytes 23044
  674.9 7.8 copy-start.8
  674.9 5.8 collective-permute-start.27
  676.9 5.8 collective-permute-start.26
  700.9 6.0 collective-permute-start.28
  702.8 5.6 collective-permute-start.29
  712.8 9.4 %all-to-all-start.14 = ((f32[4,15,128]{2,1,0:T(8,128)}), f32[4,15,128]{2,1,0:T(8,128)}, u32[]{:S(2)}, u32[]{:S(2)}) async-start(f32[4,15,128]{2,1,0:T(8,128)} %reshape.111), calls=%async_computation.14 | async-start | bytes 65536 | tf_op jit(solution)/shard_map/all_to_all | solution.py:57
  722.9 46.4 %copy-start.11 = (f32[15,128]{1,0:T(8,128)}, f32[15,128]{1,0:T(8,128)S(1)}, u32[]{:S(2)}) copy-start(f32[15,128]{1,0:T(8,128)S(1)} %reduce_sum.245) | copy-start | bytes 23044
  782.0 7.8 copy-start.9
  782.0 5.6 collective-permute-start.31
  784.0 5.8 collective-permute-start.30
  808.0 6.0 collective-permute-start.32
  809.9 5.6 collective-permute-start.33
  819.9 9.4 %all-to-all-start.16 = ((f32[4,15,128]{2,1,0:T(8,128)}), f32[4,15,128]{2,1,0:T(8,128)}, u32[]{:S(2)}, u32[]{:S(2)}) async-start(f32[4,15,128]{2,1,0:T(8,128)} %reshape.114), calls=%async_computation.16 | async-start | bytes 65536 | tf_op jit(solution)/shard_map/all_to_all | solution.py:57
where the time goes:
time: 897 us; the launch traced here: 880 us
  blocking collectives  409 us (46%)
  other arithmetic  137 us (15%)
  local copies, waits for them, and re-layouts  119 us (13%)
  starting transfers between devices  112 us (12%)
  waiting for transfers between devices  73.5 us (8%)
  between operations  30.3 us (3%)
    psum x32, blocking collectives, by_axis(): value = lax.psum(value, axis)  349 us
    all_to_all x7, blocking collectives, copy_for_each(): return lax.all_to_all(copies, axis, split_axis=0, concat_axis=0, tiled=True)  59.4 us
    scatter-add x9, other arithmetic, to_slab(): jax.ops.segment_sum(entries, targets.reshape(-1), num_segments=3 * faces_...  58.8 us
    gather x16, local copies, waits for them, and re-layouts, operate(): slab[:, local_index]  44.8 us
    ppermute x18, starting transfers between devices, shifted(): return lax.ppermute(block, axis, route)  39.9 us
    all_to_all x9, waiting for transfers between devices, summed_on_arrival(): lax.all_to_all(cut_along(value, dim, count), axis, 0, 0, tiled=True)  37.1 us
    all_to_all x9, starting transfers between devices, summed_on_arrival(): lax.all_to_all(cut_along(value, dim, count), axis, 0, 0, tiled=True)  32.8 us
    unnamed x17, other arithmetic  27.6 us
  transfers between devices with their start and end apart: 44, of which 27 were waited for; matrix products, arithmetic and copies ran while one was open for 4% of the time, Pallas kernels for 0%

commit v1 on v0

--- a/solution.py
+++ b/solution.py
@@ -7,6 +7,12 @@
 ITERS = 8
 DOM = ("dom_0", "dom_1", "dom_2")
 DOM_GRP = ("dom_0", "dom_1", "dom_2", "grp")
+
+
+def gather_and_add(x, name):
+    parts = lax.all_gather(x, name, axis=0, tiled=False)
+    summed = parts.sum(axis=0)
+    return summed
 
 
 def in_order(blocks, dim):
@@ -60,7 +66,7 @@
 
 def by_axis(value, axes):
     for axis in axes:
-        value = lax.psum(value, axis)
+        value = gather_and_add(value, axis)
     return value
 
 

time: 897 us -> 1040 us (1.16)
  local copies, waits for them, and re-layouts: 119 us -> 238 us
  other arithmetic: 137 us -> 182 us
  blocking collectives: 409 us -> 391 us
    psum x32 -> x0, blocking collectives: 349 us -> none  [by_axis(): value = lax.psum(value, axis)]
    unnamed x0 -> x32, blocking collectives: none -> 332 us
    unnamed x42 -> x194, local copies, waits for them, and re-layouts: 13.3 us -> 132 us
    reduce_sum x0 -> x64, other arithmetic: none -> 44.8 us  [gather_and_add(): summed = parts.sum(axis=0)]
where the time goes in v1:
time: 1040 us; the launch traced here: 1030 us
  blocking collectives  391 us (38%)
  local copies, waits for them, and re-layouts  238 us (23%)
  other arithmetic  182 us (18%)
  starting transfers between devices  112 us (11%)
  waiting for transfers between devices  73.8 us (7%)
  between operations  31.3 us (3%)
    unnamed x32, blocking collectives  332 us
    unnamed x194, local copies, waits for them, and re-layouts  132 us
    all_to_all x7, blocking collectives, copy_for_each(): return lax.all_to_all(copies, axis, split_axis=0, concat_axis=0, tiled=True)  59.4 us
    scatter-add x9, other arithmetic, to_slab(): jax.ops.segment_sum(entries, targets.reshape(-1), num_segments=3 * faces_...  59 us
    gather x16, local copies, waits for them, and re-layouts, operate(): slab[:, local_index]  44.8 us
    reduce_sum x64, other arithmetic, gather_and_add(): summed = parts.sum(axis=0)  44.8 us
    ppermute x18, starting transfers between devices, shifted(): return lax.ppermute(block, axis, route)  39.4 us
    all_to_all x9, waiting for transfers between devices, summed_on_arrival(): lax.all_to_all(cut_along(value, dim, count), axis, 0, 0, tiled=True)  37.1 us
  transfers between devices with their start and end apart: 44, of which 27 were waited for; matrix products, arithmetic and copies ran while one was open for 4% of the time, Pallas kernels for 0%

profile of v1, /device:TPU:8, one launch (start us, length us, event | category | flops | bytes accessed | tf_op | source)
XLA Modules:
  0.0 1028.0 jit_solution(3661521938234476110)
XLA Ops:
  15.6 3.7 all-to-all-start
  20.0 4.8 all-to-all-done
  25.4 3.3 all-to-all-start.1
  28.7 5.4 all-to-all-done.1
  44.2 3.7 gather_fusion
  53.7 7.1 scatter_custom_fusion.1
  78.8 4.0 all-to-all-done.2
  87.5 24.8 %all-reduce.71 = (f32[8]{0:T(128)S(1)}, f32[8]{0:T(128)S(1)}) all-reduce(f32[8]{0:T(128)S(1)} %dynamic-update-slice, f32[8]{0:T(128)S(1)} %dynamic-update-slice.4), channel_id=1, replica_groups=mesh['dom_0'=8,'dom_1'=4,'dom_2'=2,'grp'=4] {'dom_0'}, use_global_device_ids=true, to_apply=%add | all-reduce | flops 16 | bytes 128
  117.5 12.5 %all-reduce.87 = (f32[4]{0:T(128)S(1)}, f32[4]{0:T(128)S(1)}) all-reduce(f32[4]{0:T(128)S(1)} %dynamic-update-slice.1, f32[4]{0:T(128)S(1)} %dynamic-update-slice.5), channel_id=1, replica_groups=mesh['dom_0'=8,'dom_1'=4,'dom_2'=2,'grp'=4] {'dom_1'}, use_global_device_ids=true, to_apply=%add.1 | all-reduce | flops 8 | bytes 64
  141.0 8.9 all-reduce.79
  152.4 8.5 all_to_all.85
  170.9 3.7 gather_fusion.1
  180.5 7.1 scatter_custom_fusion.2
  203.6 4.1 all-to-all-done.4
  211.1 17.1 %all-reduce.70 = (f32[8]{0:T(128)S(1)}, f32[8]{0:T(128)S(1)}) all-reduce(f32[8]{0:T(128)S(1)} %dynamic-update-slice.8, f32[8]{0:T(128)S(1)} %dynamic-update-slice.12), channel_id=1, replica_groups=mesh['dom_0'=8,'dom_1'=4,'dom_2'=2,'grp'=4] {'dom_0'}, use_global_device_ids=true, to_apply=%add.8 | all-reduce | flops 16 | bytes 128
  232.3 11.4 %all-reduce.86 = (f32[4]{0:T(128)S(1)}, f32[4]{0:T(128)S(1)}) all-reduce(f32[4]{0:T(128)S(1)} %dynamic-update-slice.9, f32[4]{0:T(128)S(1)} %dynamic-update-slice.13), channel_id=1, replica_groups=mesh['dom_0'=8,'dom_1'=4,'dom_2'=2,'grp'=4] {'dom_1'}, use_global_device_ids=true, to_apply=%add.9 | all-reduce | flops 8 | bytes 64
  254.6 8.9 all-reduce.78
  269.3 8.5 all_to_all.86
  287.8 3.7 gather_fusion.2
  297.3 7.1 scatter_custom_fusion.3
  320.5 4.1 all-to-all-done.6
  329.3 17.1 %all-reduce.69 = (f32[8]{0:T(128)S(1)}, f32[8]{0:T(128)S(1)}) all-reduce(f32[8]{0:T(128)S(1)} %dynamic-update-slice.16, f32[8]{0:T(128)S(1)} %dynamic-update-slice.20), channel_id=1, replica_groups=mesh['dom_0'=8,'dom_1'=4,'dom_2'=2,'grp'=4] {'dom_0'}, use_global_device_ids=true, to_apply=%add.16 | all-reduce | flops 16 | bytes 128
  350.2 11.4 %all-reduce.85 = (f32[4]{0:T(128)S(1)}, f32[4]{0:T(128)S(1)}) all-reduce(f32[4]{0:T(128)S(1)} %dynamic-update-slice.17, f32[4]{0:T(128)S(1)} %dynamic-update-slice.21), channel_id=1, replica_groups=mesh['dom_0'=8,'dom_1'=4,'dom_2'=2,'grp'=4] {'dom_1'}, use_global_device_ids=true, to_apply=%add.17 | all-reduce | flops 8 | bytes 64
  372.2 8.9 all-reduce.77
  387.0 8.5 all_to_all.87
  406.9 3.7 gather_fusion.3
  416.4 7.1 scatter_custom_fusion.4
  436.3 3.9 all-to-all-start.8
  441.5 4.2 all-to-all-done.8
  449.9 17.1 %all-reduce.68 = (f32[8]{0:T(128)S(1)}, f32[8]{0:T(128)S(1)}) all-reduce(f32[8]{0:T(128)S(1)} %dynamic-update-slice.24, f32[8]{0:T(128)S(1)} %dynamic-update-slice.28), channel_id=1, replica_groups=mesh['dom_0'=8,'dom_1'=4,'dom_2'=2,'grp'=4] {'dom_0'}, use_global_device_ids=true, to_apply=%add.24 | all-reduce | flops 16 | bytes 128
  470.9 11.4 %all-reduce.84 = (f32[4]{0:T(128)S(1)}, f32[4]{0:T(128)S(1)}) all-reduce(f32[4]{0:T(128)S(1)} %dynamic-update-slice.25, f32[4]{0:T(128)S(1)} %dynamic-update-slice.29), channel_id=1, replica_groups=mesh['dom_0'=8,'dom_1'=4,'dom_2'=2,'grp'=4] {'dom_1'}, use_global_device_ids=true, to_apply=%add.25 | all-reduce | flops 8 | bytes 64
  492.7 8.9 all-reduce.76
  506.7 8.5 all_to_all.88
  526.6 3.7 gather_fusion.4
  536.1 7.1 scatter_custom_fusion.5
  555.9 4.3 all-to-all-start.10
  561.6 4.1 all-to-all-done.10
  571.6 17.2 %all-reduce.67 = (f32[8]{0:T(128)S(1)}, f32[8]{0:T(128)S(1)}) all-reduce(f32[8]{0:T(128)} %dynamic-update-slice.32, f32[8]{0:T(128)} %copy-done.19), channel_id=1, replica_groups=mesh['dom_0'=8,'dom_1'=4,'dom_2'=2,'grp'=4] {'dom_0'}, use_global_device_ids=true, to_apply=%add.32 | all-reduce | flops 16 | bytes 128
  594.5 11.6 %all-reduce.83 = (f32[4]{0:T(128)S(1)}, f32[4]{0:T(128)S(1)}) all-reduce(f32[4]{0:T(128)} %dynamic-update-slice.33, f32[4]{0:T(128)} %copy-done.20), channel_id=1, replica_groups=mesh['dom_0'=8,'dom_1'=4,'dom_2'=2,'grp'=4] {'dom_1'}, use_global_device_ids=true, to_apply=%add.33 | all-reduce | flops 8 | bytes 64
  620.0 9.0 all-reduce.75
  635.0 8.5 all_to_all.89
  654.8 3.7 gather_fusion.5
  664.4 7.1 scatter_custom_fusion.6
  684.2 3.9 all-to-all-start.12
  689.4 4.2 all-to-all-done.12
  700.8 17.2 %all-reduce.66 = (f32[8]{0:T(128)S(1)}, f32[8]{0:T(128)S(1)}) all-reduce(f32[8]{0:T(128)} %dynamic-update-slice.40, f32[8]{0:T(128)} %copy-done.23), channel_id=1, replica_groups=mesh['dom_0'=8,'dom_1'=4,'dom_2'=2,'grp'=4] {'dom_0'}, use_global_device_ids=true, to_apply=%add.40 | all-reduce | flops 16 | bytes 128
  723.5 11.6 %all-reduce.82 = (f32[4]{0:T(128)S(1)}, f32[4]{0:T(128)S(1)}) all-reduce(f32[4]{0:T(128)} %dynamic-update-slice.41, f32[4]{0:T(128)} %copy-done.24), channel_id=1, replica_groups=mesh['dom_0'=8,'dom_1'=4,'dom_2'=2,'grp'=4] {'dom_1'}, use_global_device_ids=true, to_apply=%add.41 | all-reduce | flops 8 | bytes 64
  748.7 9.0 all-reduce.74
  762.9 8.5 all_to_all.90
  782.7 3.7 gather_fusion.6
  792.3 7.2 scatter_custom_fusion.7
  812.3 3.9 all-to-all-start.14
  817.5 4.2 all-to-all-done.14
  829.3 17.8 %all-reduce.65 = (f32[8]{0:T(128)}, f32[8]{0:T(128)}) all-reduce(f32[8]{0:T(128)} %dynamic-update-slice.48, f32[8]{0:T(128)} %dynamic-update-slice.52), channel_id=1, replica_groups=mesh['dom_0'=8,'dom_1'=4,'dom_2'=2,'grp'=4] {'dom_0'}, use_global_device_ids=true, to_apply=%add.48 | all-reduce | flops 16 | bytes 128
  855.7 12.1 %all-reduce.81 = (f32[4]{0:T(128)}, f32[4]{0:T(128)}) all-reduce(f32[4]{0:T(128)} %dynamic-update-slice.49, f32[4]{0:T(128)} %dynamic-update-slice.53), channel_id=1, replica_groups=mesh['dom_0'=8,'dom_1'=4,'dom_2'=2,'grp'=4] {'dom_1'}, use_global_device_ids=true, to_apply=%add.49 | all-reduce | flops 8 | bytes 64
  888.3 9.6 all-reduce.73
  905.3 8.5 all_to_all.91
  925.2 3.7 gather_fusion.7
  934.7 7.1 scatter_custom_fusion.8
  954.5 3.9 all-to-all-start.16
  960.4 3.6 all-to-all-done.16
  968.8 17.1 %all-reduce.64 = (f32[8]{0:T(128)S(1)}, f32[8]{0:T(128)S(1)}) all-reduce(f32[8]{0:T(128)S(1)} %dynamic-update-slice.56, f32[8]{0:T(128)S(1)} %dynamic-update-slice.60), channel_id=1, replica_groups=mesh['dom_0'=8,'dom_1'=4,'dom_2'=2,'grp'=4] {'dom_0'}, use_global_device_ids=true, to_apply=%add.56 | all-reduce | flops 16 | bytes 128
  989.7 11.4 %all-reduce.80 = (f32[4]{0:T(128)S(1)}, f32[4]{0:T(128)S(1)}) all-reduce(f32[4]{0:T(128)S(1)} %dynamic-update-slice.57, f32[4]{0:T(128)S(1)} %dynamic-update-slice.61), channel_id=1, replica_groups=mesh['dom_0'=8,'dom_1'=4,'dom_2'=2,'grp'=4] {'dom_1'}, use_global_device_ids=true, to_apply=%add.57 | all-reduce | flops 8 | bytes 64
  1011.5 8.9 all-reduce.72
  (482 shorter events, 470.8 us)
Async XLA Ops:
  0.6 1.9 copy-start
  6.8 5.0 collective-permute-start
  8.7 6.1 collective-permute-start.1
  11.8 168.7 %copy-start.16 = (s32[896]{0:T(1024)}, s32[896]{0:T(1024)S(1)}, u32[]{:S(2)}) copy-start(s32[896]{0:T(1024)S(1)} %get-tuple-element.109) | copy-start | bytes 10756
  15.6 9.2 all-to-all-start
  25.4 8.7 all-to-all-start.1
  34.8 7.4 collective-permute-start.3
  36.7 5.8 collective-permute-start.2
  42.2 24.9 %copy-start.18 = (u32[256]{0:T(256)S(1)}, u32[256]{0:T(256)}, u32[]{:S(2)}) copy-start(u32[256]{0:T(256)} %constant.35) | copy-start | bytes 3076
  42.2 35.2 %copy-start.1 = (f32[7,15,60,128]{3,2,1,0:T(8,128)S(1)}, f32[7,15,60,128]{3,2,1,0:T(8,128)}, u32[]{:S(2)}) copy-start(f32[7,15,60,128]{3,2,1,0:T(8,128)} %param.14) | copy-start | bytes 9676804
  49.8 33.1 %copy-start.2 = (f32[15,128]{1,0:T(8,128)S(1)}, f32[15,128]{1,0:T(8,128)}, u32[]{:S(2)}) copy-start(f32[15,128]{1,0:T(8,128)} %param.15) | copy-start | bytes 23044
  49.8 84.4 %copy-start.17 = (u32[256]{0:T(256)S(1)}, u32[256]{0:T(256)}, u32[]{:S(2)}) copy-start(u32[256]{0:T(256)} %constant.50) | copy-start | bytes 3076
  62.3 7.1 collective-permute-start.4
  65.2 5.9 collective-permute-start.5
  74.2 8.7 all-to-all-start.2
  162.4 7.8 copy-start.3
  162.4 5.7 collective-permute-start.7
  164.4 5.8 collective-permute-start.6
  188.4 6.0 collective-permute-start.8
  190.3 5.6 collective-permute-start.9
  199.0 8.7 all-to-all-start.4
  208.3 85.1 %copy-start.13 = (f32[15,128]{1,0:T(8,128)}, f32[15,128]{1,0:T(8,128)S(1)}, u32[]{:S(2)}) copy-start(f32[15,128]{1,0:T(8,128)S(1)} %get-tuple-element.88) | copy-start | bytes 23044
  279.3 7.8 copy-start.4
  279.3 5.6 collective-permute-start.11
  281.3 5.8 collective-permute-start.10
  305.3 6.0 collective-permute-start.12
  307.2 5.6 collective-permute-start.13
  315.8 8.7 all-to-all-start.6
  387.0 119.7 %copy-start.15 = (f32[15,128]{1,0:T(8,128)}, f32[15,128]{1,0:T(8,128)S(1)}, u32[]{:S(2)}) copy-start(f32[15,128]{1,0:T(8,128)S(1)} %get-tuple-element.87) | copy-start | bytes 23044
  398.4 7.8 copy-start.5
  398.4 5.6 collective-permute-start.15
  400.4 5.8 collective-permute-start.14
  424.4 6.0 collective-permute-start.16
  426.3 5.6 collective-permute-start.17
  436.3 9.4 all-to-all-start.8
  518.0 7.8 copy-start.6
  518.0 5.6 collective-permute-start.19
  520.1 5.8 collective-permute-start.18
  544.1 6.0 collective-permute-start.20
  546.0 5.6 collective-permute-start.21
  555.9 9.8 all-to-all-start.10
  566.5 67.1 %copy-start.14 = (f32[15,128]{1,0:T(8,128)}, f32[15,128]{1,0:T(8,128)S(1)}, u32[]{:S(2)}) copy-start(f32[15,128]{1,0:T(8,128)S(1)} %reduce_sum.851) | copy-start | bytes 23044
  590.8 1.2 copy-start.20
  635.0 127.9 %copy-start.12 = (f32[15,128]{1,0:T(8,128)}, f32[15,128]{1,0:T(8,128)S(1)}, u32[]{:S(2)}) copy-start(f32[15,128]{1,0:T(8,128)S(1)} %get-tuple-element.84) | copy-start | bytes 23044
  646.3 7.8 copy-start.7
  646.3 5.6 collective-permute-start.23
  648.4 5.8 collective-permute-start.22
  672.3 6.0 collective-permute-start.24
  674.3 5.6 collective-permute-start.25
  684.2 9.4 all-to-all-start.12
  696.3 92.0 %copy-start.10 = (f32[15,128]{1,0:T(8,128)}, f32[15,128]{1,0:T(8,128)S(1)}, u32[]{:S(2)}) copy-start(f32[15,128]{1,0:T(8,128)S(1)} %get-tuple-element.82) | copy-start | bytes 23044
  774.2 7.8 copy-start.8
  774.2 5.6 collective-permute-start.27
  776.2 5.8 collective-permute-start.26
  800.4 6.0 collective-permute-start.28
  802.3 5.6 collective-permute-start.29
  812.3 9.4 all-to-all-start.14
  822.4 81.4 %copy-start.11 = (f32[15,128]{1,0:T(8,128)}, f32[15,128]{1,0:T(8,128)S(1)}, u32[]{:S(2)}) copy-start(f32[15,128]{1,0:T(8,128)S(1)} %reduce_sum.873) | copy-start | bytes 23044
  916.6 7.8 copy-start.9
  916.6 5.6 collective-permute-start.31
  918.7 5.8 collective-permute-start.30
  942.6 6.0 collective-permute-start.32
  944.6 5.6 collective-permute-start.33
  954.5 9.4 all-to-all-start.16
  (7 other events, 6.8 us)
